TPU v7x, 32 devices: a whole 2x2x4 slice. The times are simulated.
32 devices in a mesh: cuts: 16 (over z, x, core), ang: 2 (over y).
Axes of the slice: x: 2, y: 2, z: 4, core: 2. Of those that a mesh axis runs over, the one named last changes fastest.
Arguments:
- projections: bfloat16 [16, 16, 2, 128, 256], P('cuts', None, 'ang'), may hold values from -48 to 48
- start_image: bfloat16 [4096, 1024], P('cuts'), may hold values from 0 to 2
- system: bfloat16 [8, 16, 2, 64, 128], P('ang'), may hold values from 0.0009994507 to 0.029907227
- first_tile: int32 [8, 16], P('ang'), may hold values from 0 to 3, as said below
Outputs:
- new_image: float32 [4096, 1024], P('cuts', 'ang')
- residual: bfloat16 [16, 4096, 256], P('ang', 'cuts')
Inputs may be any that keep to these rules, and one draw needn't show every extreme that they name: In every angle block each bin tile is first_tile of at least one pixel tile; every pixel tile meets exactly two bin tiles, first_tile and first_tile + 1 modulo 4.
All inputs are finite; a program needn't handle non-finite values.
Results may differ from a plain program's by a relative error of at most 0.001.
Values may be sent and summed in bfloat16 or wider, within the bound.
A program may use at most 128 MiB of HBM per device.

v0:
```python
import jax
import jax.numpy as jnp
from jax import lax
from jax.sharding import PartitionSpec as P


def on_device(projections, start_image, system, first_tile):
    arrived = lax.all_to_all(
        lax.all_to_all(projections, "cuts", split_axis=1, concat_axis=0, tiled=True),
        "ang",
        split_axis=0,
        concat_axis=2,
        tiled=True,
    )
    blocks = system.shape[0]
    pix_tiles = system.shape[1]
    tile_len = system.shape[3]
    pair_len = system.shape[4] // tile_len
    bin_tiles = arrived.shape[-1] // tile_len
    slices = start_image.shape[0]
    npixels = pix_tiles * tile_len
    highest = lax.Precision.HIGHEST
    tile_ids = jnp.arange(bin_tiles, dtype=jnp.int32)
    bin_index = jnp.stack([first_tile, (first_tile + 1) % bin_tiles], axis=2)
    onehot = (bin_index[..., None] == tile_ids).astype(jnp.float32)
    pixels = start_image.reshape(slices, pix_tiles, tile_len)
    partial_value = jnp.einsum(
        "spi,gpjic->gpjsc", pixels, system, preferred_element_type=jnp.float32
    )
    forward = jnp.einsum(
        "gpjb,gpjsc->gbsc",
        onehot,
        partial_value,
        precision=highest,
        preferred_element_type=jnp.float32,
    )
    ray_weights = jnp.sum(system, axis=3, dtype=jnp.float32)
    row_total = jnp.einsum(
        "gpjb,gpjc->gbc", onehot, ray_weights, precision=highest, preferred_element_type=jnp.float32
    )
    col_part = jnp.sum(system, axis=(0, 2, 4), dtype=jnp.float32).reshape(npixels)
    sinogram = arrived.reshape(blocks, pair_len, slices, bin_tiles, tile_len)
    sinogram = sinogram.transpose(0, 3, 2, 1, 4).reshape(
        blocks, bin_tiles, slices, pair_len * tile_len
    )
    resid_tiles = ((sinogram.astype(jnp.float32) - forward) / row_total[:, :, None, :]).astype(
        jnp.bfloat16
    )
    picked = jnp.einsum(
        "gpjb,gbsc->gpjsc",
        onehot.astype(jnp.bfloat16),
        resid_tiles,
        preferred_element_type=jnp.float32,
    ).astype(jnp.bfloat16)
    backproj = jnp.einsum(
        "gpjsc,gpjic->spi", picked, system, preferred_element_type=jnp.float32
    ).reshape(slices, npixels)
    share_len = npixels // lax.axis_size("ang")
    offset = lax.axis_index("ang") * share_len
    summed, columns = (
        lax.psum_scatter(backproj, "ang", scatter_dimension=1, tiled=True),
        lax.psum_scatter(col_part, "ang", scatter_dimension=0, tiled=True),
    )
    local_image = lax.dynamic_slice_in_dim(start_image, offset, share_len, 1).astype(jnp.float32)
    new_image = local_image + summed / columns[None, :]
    residual = resid_tiles.reshape(blocks, bin_tiles, slices, pair_len, tile_len)
    residual = residual.transpose(0, 3, 2, 1, 4).reshape(
        blocks * pair_len, slices, bin_tiles * tile_len
    )
    return (new_image, residual)


def solution(mesh):
    in_specs = (
        P("cuts", None, "ang", None, None),
        P("cuts", None),
        P("ang", None, None, None, None),
        P("ang", None),
    )
    out_specs = (P("cuts", "ang"), P("ang", "cuts", None))
    return jax.shard_map(
        on_device, mesh=mesh, in_specs=in_specs, out_specs=out_specs, check_vma=False
    )
```

profile of v0, /device:TPU:0, one launch (start us, length us, event | category | flops | bytes accessed | tf_op | source)
XLA Modules:
  0.0 123.1 jit_solution(408915117770366399)
XLA Ops:
  7.2 0.0 copy-start
  7.2 7.5 %all-to-all-start = ((bf16[1,16,1,128,256]{4,3,2,0,1:T(8,128)(2,1)}), bf16[1,16,1,128,256]{4,3,2,0,1:T(8,128)(2,1)S(1)}, u32[]{:S(2)}, u32[]{:S(2)}) async-start(bf16[1,16,1,128,256]{4,3,2,0,1:T(8,128)(2,1)} %bitcast.68), calls=%async_computation | async-start | bytes 2097152 | tf_op jit(solution)/shard_map/all_to_all | solution.py:9
  14.7 2.0 %copy.25 = bf16[256,1024]{0,1:T(8,128)(2,1)} copy(bf16[256,1024]{1,0:T(8,128)(2,1)} %param.5) | data formatting | bytes 1048576 | tf_op args[1]
  16.8 9.1 %convolution_bitcast_fusion = f32[4,16,2,256,128]{3,4,2,0,1:T(8,128)} fusion(bf16[256,16,64,1,1]{0,2,4,3,1:T(8,128)(2,1)} %bitcast.67, bf16[4,16,2,64,128]{4,3,2,1,0:T(8,128)(2,1)S(1)} %copy-done), kind=kOutput, calls=%fused_computation | convolution fusion | flops 536870912 | bytes 19398656 | tf_op jit(solution)/shard_map/spi,gpjic->gpjsc/dot_general | solution.py:27
  25.9 11.7 %all-to-all-done = bf16[1,16,1,128,256]{4,3,2,0,1:T(8,128)(2,1)S(1)} async-done(((bf16[1,16,1,128,256]{4,3,2,0,1:T(8,128)(2,1)}), bf16[1,16,1,128,256]{4,3,2,0,1:T(8,128)(2,1)S(1)}, u32[]{:S(2)}, u32[]{:S(2)}) %all-to-all-start) | async-done | bytes 1048608 | tf_op jit(solution)/shard_map/all_to_all | solution.py:9
  37.6 1.0 copy-done.2
  38.6 3.6 %all-to-all-start.1 = ((bf16[16,1,1,128,256]{4,3,2,1,0:T(8,128)(2,1)}), bf16[16,1,1,128,256]{4,3,2,1,0:T(8,128)(2,1)S(1)}, u32[]{:S(2)}, u32[]{:S(2)}) async-start(bf16[16,1,1,128,256]{4,3,2,1,0:T(8,128)(2,1)} %bitcast.64), calls=%async_computation.1 | async-start | bytes 2097152 | tf_op jit(solution)/shard_map/all_to_all | solution.py:8
  42.2 0.2 reduce-scatter.2.cloned.1.call-start
  42.4 20.2 %copy.27 = f32[4,16,2,256,128]{4,1,2,3,0:T(8,128)} copy(f32[4,16,2,256,128]{3,4,2,0,1:T(8,128)} %convolution_bitcast_fusion) | data formatting | bytes 33554432 | tf_op jit(solution)/shard_map/spi,gpjic->gpjsc/transpose | solution.py:27
  62.6 0.6 convert_reduce_fusion
  63.3 0.2 convolution_bitcast_fusion.1
  63.5 0.8 copy.23
  64.3 2.7 %reshape.38 = f32[4,2,256,4,64]{2,4,3,1,0:T(8,128)} reshape(f32[8,1,2,1,128,256]{4,2,5,0,3,1:T(2,128)S(1)} %bitcast.60) | data formatting | bytes 4194304 | tf_op jit(solution)/shard_map/convert_element_type | solution.py:46
  67.1 3.1 %copy.24 = f32[4,4,256,2,64]{2,4,3,1,0:T(8,128)} copy(f32[4,4,256,2,64]{2,4,1,3,0:T(8,128)} %bitcast.61) | data formatting | bytes 4194304 | tf_op jit(solution)/shard_map/convert_element_type | solution.py:46
  70.2 2.0 %copy.28 = f32[4,4,256,128]{3,1,2,0:T(4,128)S(1)} copy(f32[4,4,256,128]{2,3,1,0:T(8,128)} %bitcast.62) | data formatting | bytes 4194304 | tf_op jit(solution)/shard_map/convert_element_type | solution.py:46
  72.2 9.9 %fusion.3 = bf16[4,4,256,128]{3,1,2,0:T(4,128)(2,1)S(1)} fusion(f32[4,4,256,128]{3,1,2,0:T(4,128)S(1)} %copy.28, f32[4,16,2,256,128]{4,1,2,3,0:T(8,128)} %copy.27, f32[4,4,128]{2,1,0:T(4,128)S(1)} %convolution_bitcast_fusion.1, s32[4,16,2]{1,2,0:T(2,128)S(1)} %copy.20), kind=kOutput, calls=%fused_computation.8 | convolution fusion | flops 202899968 | bytes 19931648 | tf_op jit(solution)/shard_map/gpjb,gpjsc->gbsc/dot_general | solution.py:30
  82.1 0.0 copy-start.1
  82.1 3.0 %convolution_convert_fusion = bf16[4,16,2,256,128]{4,1,3,2,0:T(8,128)(2,1)S(1)} fusion(bf16[4,4,256,128]{3,1,2,0:T(4,128)(2,1)S(1)} %fusion.3, s32[4,16,2]{1,2,0:T(2,128)S(1)} %copy.20), kind=kOutput, calls=%fused_computation.3 | convolution fusion | flops 37750272 | bytes 9437696 | tf_op jit(solution)/shard_map/gpjb,gbsc->gpjsc/dot_general | solution.py:49
  85.1 5.0 %fusion = f32[16,256,64,1,1]{1,2,4,3,0:T(8,128)S(1)} fusion(bf16[4,16,2,256,128]{4,1,3,2,0:T(8,128)(2,1)S(1)} %convolution_convert_fusion, bf16[4,16,2,64,128]{4,3,2,1,0:T(8,128)(2,1)S(1)} %copy-done.1), kind=kOutput, calls=%fused_computation.1 | convolution fusion | flops 536870912 | bytes 11534336 | tf_op jit(solution)/shard_map/gpjsc,gpjic->spi/dot_general | solution.py:55
  90.1 0.0 copy-start.5
  90.1 1.3 %copy.31 = f32[256,1024]{1,0:T(8,128)} copy(f32[256,1024]{0,1:T(8,128)S(1)} %bitcast.69) | data formatting | bytes 2097152 | tf_op jit(solution)/shard_map/reshape | solution.py:57
  91.4 0.0 reduce-scatter.2.cloned.1.call-update
  91.5 0.1 reshape.34
  91.5 0.6 dynamic-slice
  92.8 4.9 %all-reduce = f32[1024]{0:T(1024)S(1)} all-reduce(f32[1024]{0:T(1024)S(1)} %reshape.34), channel_id=3, replica_groups=mesh['cuts'=16,'ang'=2] {'ang'}, use_global_device_ids=true, to_apply=%region_3.4.clone | all-reduce | flops 1024 | bytes 8192
  97.7 0.1 dynamic-slice.1
  97.8 0.6 copy.32
  98.4 0.0 copy-start.3
  98.4 0.1 copy.33
  98.5 1.3 %copy.34 = bf16[8,256,256]{2,1,0:T(8,128)(2,1)} copy(bf16[8,256,256]{1,2,0:T(8,128)(2,1)S(1)} %bitcast.66) | data formatting | bytes 2097152
  99.8 14.6 %reduce-scatter.2.cloned.1.call-done = f32[256,512]{1,0:T(8,128)} async-done(((f32[256,1024]{1,0:T(8,128)}), f32[256,512]{1,0:T(8,128)}) %reduce-scatter.2.cloned.1.call-update) | async-done | bytes 524304 | tf_op jit(solution)/shard_map/reduce_scatter | solution.py:61
  114.4 1.9 %divide_add_fusion = f32[256,512]{1,0:T(8,128)} fusion(f32[256,512]{1,0:T(8,128)} %reduce-scatter.2.cloned.1.call-done, f32[512]{0:T(512)S(1)} %dynamic-slice.1, bf16[256,1024]{1,0:T(8,128)(2,1)S(1)} %copy-done.3, s32[]{:T(128)S(6)} %select_n.10), kind=kLoop, calls=%fused_computation.13 | loop fusion | flops 393216 | bytes 1312772 | tf_op jit(solution)/shard_map/add | solution.py:65
  (11 shorter events, 0.0 us)
Async XLA Ops:
  7.2 9.6 %copy-start = (bf16[4,16,2,64,128]{4,3,2,1,0:T(8,128)(2,1)S(1)}, bf16[4,16,2,64,128]{4,3,2,1,0:T(8,128)(2,1)}, u32[]{:S(2)}) copy-start(bf16[4,16,2,64,128]{4,3,2,1,0:T(8,128)(2,1)} %param.6) | copy-start | bytes 6291460
  7.2 30.4 %all-to-all-start = ((bf16[1,16,1,128,256]{4,3,2,0,1:T(8,128)(2,1)}), bf16[1,16,1,128,256]{4,3,2,0,1:T(8,128)(2,1)S(1)}, u32[]{:S(2)}, u32[]{:S(2)}) async-start(bf16[1,16,1,128,256]{4,3,2,0,1:T(8,128)(2,1)} %bitcast.68), calls=%async_computation | async-start | bytes 2097152 | tf_op jit(solution)/shard_map/all_to_all | solution.py:9
  25.9 16.5 %copy-start.4 = (s32[4,16]{1,0:T(4,128)S(1)}, s32[4,16]{1,0:T(4,128)}, u32[]{:S(2)}) copy-start(s32[4,16]{1,0:T(4,128)} %param.7) | copy-start | bytes 772
  37.6 1.0 copy-start.2
  38.6 24.9 %all-to-all-start.1 = ((bf16[16,1,1,128,256]{4,3,2,1,0:T(8,128)(2,1)}), bf16[16,1,1,128,256]{4,3,2,1,0:T(8,128)(2,1)S(1)}, u32[]{:S(2)}, u32[]{:S(2)}) async-start(bf16[16,1,1,128,256]{4,3,2,1,0:T(8,128)(2,1)} %bitcast.64), calls=%async_computation.1 | async-start | bytes 2097152 | tf_op jit(solution)/shard_map/all_to_all | solution.py:8
  42.2 72.2 %reduce-scatter.2.cloned.1.call-start = ((), (), s32[]{:S(2)}) async-start(), calls=%async_computation.3 | async-start | bytes 1572864 | tf_op jit(solution)/shard_map/reduce_scatter | solution.py:61
  82.1 3.0 %copy-start.1 = (bf16[4,16,2,64,128]{4,3,2,1,0:T(8,128)(2,1)S(1)}, bf16[4,16,2,64,128]{4,3,2,1,0:T(8,128)(2,1)}, u32[]{:S(2)}) copy-start(bf16[4,16,2,64,128]{4,3,2,1,0:T(8,128)(2,1)} %param.6) | copy-start | bytes 6291460
  90.1 1.4 %copy-start.5 = (u32[32]{0:T(128)S(1)}, u32[32]{0:T(128)}, u32[]{:S(2)}) copy-start(u32[32]{0:T(128)} %constant.31) | copy-start | bytes 388
  98.4 16.0 %copy-start.3 = (bf16[256,1024]{1,0:T(8,128)(2,1)S(1)}, bf16[256,1024]{1,0:T(8,128)(2,1)}, u32[]{:S(2)}) copy-start(bf16[256,1024]{1,0:T(8,128)(2,1)} %param.5) | copy-start | bytes 1572868
Sparse Core Ops, SparseCore 0:
  91.6 22.7 reduce-scatter.1
where the time goes:
time: 124 us; the launch traced here: 123 us
  local copies, waits for them, and re-layouts  35.9 us (29%)
  matrix products  27.2 us (22%)
  waiting for transfers between devices  26.3 us (21%)
  between operations  14.8 us (12%)
  starting transfers between devices  11.3 us (9%)
  blocking collectives  4.94 us (4%)
  other arithmetic  2.59 us (2%)
    transpose x1, local copies, waits for them, and re-layouts, on_device(): jnp.einsum('spi,gpjic->gpjsc', pixels, system, preferred_element_type=jnp...  20.2 us
    reduce_scatter x1, waiting for transfers between devices, on_device(): lax.psum_scatter(backproj, 'ang', scatter_dimension=1, tiled=True)  14.6 us
    all_to_all x1, waiting for transfers between devices, on_device(): lax.all_to_all(projections, 'cuts', split_axis=1, concat_axis=0, tiled=True)  11.7 us
    dot_general x1, matrix products, on_device(): jnp.einsum('gpjb,gpjsc->gbsc', onehot, partial_value, precision=highest,...  9.9 us
    dot_general x1, matrix products, on_device(): jnp.einsum('spi,gpjic->gpjsc', pixels, system, preferred_element_type=jnp...  9.14 us
    convert_element_type x4, local copies, waits for them, and re-layouts, on_device(): sinogram.astype(jnp.float32) - forward  8.67 us
    all_to_all x1, starting transfers between devices, on_device(): lax.all_to_all(projections, 'cuts', split_axis=1, concat_axis=0, tiled=True)  7.53 us
    unnamed x16, local copies, waits for them, and re-layouts  5.01 us
  transfers between devices with their start and end apart: 3, of which 2 were waited for; matrix products, arithmetic and copies ran while one was open for 28% of the time, Pallas kernels for 0%

commit v1 on v0

v1 whole, which is shorter than its diff:
```python
import functools

import jax
import jax.numpy as jnp
from jax import lax
from jax.experimental import pallas as pl
from jax.experimental.pallas import tpu as pltpu
from jax.sharding import PartitionSpec as P

MESH = pl.DeviceIdType.MESH
NT = (((1,), (1,)), ((), ()))
MAX_CHUNKS = 4


def kernel(
    C, G, NC, first, proj, image, system, new_out, res_out,
    img, sysv, A, F, inv, hop, arr, R, U, own, urecv, colp, crecv, newv,
    img_sem, sys_sem, send_sem, hop_sem, fwd_sem, arr_sem,
    usend_sem, urecv_sem, csend_sem, crecv_sem, res_sem, new_sem,
):
    c = lax.axis_index("cuts")
    a = lax.axis_index("ang")
    T = C // G
    blocks, ptiles, _, W, PW = system.shape
    KR = proj.shape[3]
    kc = KR // NC
    rows = G * kc
    npix = image.shape[1]
    share = npix // G
    bins = proj.shape[4]
    half = bins // PW
    ntiles = bins // W

    barrier = pltpu.get_barrier_semaphore()
    for s in range(1, C):
        pl.semaphore_signal(barrier, inc=1, device_id=(lax.rem(c + s, C), a), device_id_type=MESH)
    for s in range(1, G):
        pl.semaphore_signal(barrier, inc=1, device_id=(c, lax.rem(a + s, G)), device_id_type=MESH)

    sys_copy = pltpu.make_async_copy(system, sysv, sys_sem)
    sys_copy.start()
    img_copies = []
    for q in range(NC):
        for b in range(G):
            cp = pltpu.make_async_copy(
                image.at[pl.ds(b * KR + q * kc, kc)], img.at[q, b], img_sem.at[q, b]
            )
            cp.start()
            img_copies.append(cp)
    for q in range(NC):
        pltpu.make_async_copy(
            proj.at[0, c, 0, pl.ds(q * kc, kc)], hop.at[q, c], hop_sem.at[q]
        ).start()

    pl.semaphore_wait(barrier, C - 1 + G - 1)

    for q in range(NC):
        for s in range(1, C):
            o = lax.rem(c + s, C)
            pltpu.make_async_remote_copy(
                src_ref=proj.at[0, o, 0, pl.ds(q * kc, kc)],
                dst_ref=hop.at[q, c],
                send_sem=send_sem,
                recv_sem=hop_sem.at[q],
                device_id=(o, a),
                device_id_type=MESH,
            ).start()

    sys_copy.wait()


    def build(p, carry):
        rows_p = pl.ds(pl.multiple_of(p * W, W), W)
        for g in range(blocks):
            f = first[g, p]
            w = [sysv[g, p, j].astype(jnp.float32) for j in range(2)]
            r = [pltpu.roll(x, W, 1) for x in w]
            up = (lax.broadcasted_iota(jnp.int32, (W, PW), 1) // W)
            for t in range(PW // W):
                x = [jnp.where(up == t, w[j], r[j]) for j in range(2)]
                for h in range(half):
                    b = up + h * (PW // W)
                    second = lax.rem(f + 1, ntiles)
                    tile = jnp.where(b == f, x[0], jnp.where(b == second, x[1], 0.0))
                    A[g * (PW // W) + t, rows_p, pl.ds(h * PW, PW)] = tile.astype(jnp.bfloat16)
        return carry

    lax.fori_loop(0, ptiles, build, 0)

    colp[...] = jnp.zeros_like(colp)
    for cp in img_copies:
        cp.wait()

    def project(t, carry):
        m = A[t]
        F[t] = jnp.dot(
            img[...].reshape(NC * rows, npix), m, preferred_element_type=jnp.float32
        )
        ones_r = jnp.ones((16, npix), jnp.bfloat16)
        ones_b = jnp.ones((16, bins), jnp.bfloat16)
        inv[t] = 1.0 / jnp.dot(ones_r, m, preferred_element_type=jnp.float32)[:8]
        for g in range(G):
            colp[g] += lax.dot_general(
                ones_b, A[t, pl.ds(g * share, share)], NT, preferred_element_type=jnp.float32
            )[:8]
        return carry

    lax.fori_loop(0, T, project, 0)

    for s in range(1, G):
        g = lax.rem(a + s, G)
        pltpu.make_async_remote_copy(
            src_ref=colp.at[g], dst_ref=crecv.at[s - 1], send_sem=csend_sem.at[s - 1],
            recv_sem=crecv_sem, device_id=(c, g), device_id_type=MESH,
        ).start()

    def forward_on(q):
        pltpu.make_async_copy(hop.at[q], hop.at[q], hop_sem.at[q]).wait()
        for s in range(1, G):
            g = lax.rem(a + s, G)
            pltpu.make_async_remote_copy(
                src_ref=hop.at[q, pl.ds(g * T, T)],
                dst_ref=arr.at[q, s - 1],
                send_sem=fwd_sem.at[q, s - 1],
                recv_sem=arr_sem.at[q, s - 1],
                device_id=(c, g),
                device_id_type=MESH,
            ).start()

    def res_copies(q):
        out = []
        for b in range(G):
            out.append(pltpu.make_async_copy(
                R.at[q, :, b], res_out.at[:, pl.ds(b * KR + q * kc, kc)], res_sem.at[q, b]
            ))
        return out

    def new_copies(q):
        return [
            pltpu.make_async_copy(
                newv.at[q, b], new_out.at[pl.ds(b * KR + q * kc, kc)], new_sem.at[q, b]
            )
            for b in range(G)
        ]

    def residual_part(q, b, source):
        def body(t, carry):
            value = source(t).astype(jnp.float32)
            f = F[t, pl.ds(pl.multiple_of(q * rows + b * kc, kc), kc)]
            R[q, t, b] = ((value - f) * inv[t][:1]).astype(jnp.bfloat16)
            return carry

        lax.fori_loop(0, T, body, 0)

    def back(q, g):
        total = jnp.zeros((rows, share), jnp.float32)
        pix = pl.ds(pl.multiple_of(g * share, share), share)
        for t in range(T):
            total = total + lax.dot_general(
                R[q, t].reshape(rows, bins), A[t, pix], NT, preferred_element_type=jnp.float32
            )
        return total

    def u_copy(q, s):
        g = lax.rem(a + s, G)
        return pltpu.make_async_remote_copy(
            src_ref=U.at[q, s - 1], dst_ref=urecv.at[q, s - 1],
            send_sem=usend_sem.at[q, s - 1], recv_sem=urecv_sem.at[q, s - 1],
            device_id=(c, g), device_id_type=MESH,
        )

    def process(q):
        residual_part(q, a, lambda t: hop[q, a * T + t])
        for s in range(1, G):
            pltpu.make_async_copy(arr.at[q, s - 1], arr.at[q, s - 1], arr_sem.at[q, s - 1]).wait()
            residual_part(q, lax.rem(a + G - s, G), lambda t, s=s: arr[q, s - 1, t])
        for cp in res_copies(q):
            cp.start()
        for s in range(1, G):
            U[q, s - 1] = back(q, lax.rem(a + s, G))
            u_copy(q, s).start()
        own[q] = back(q, a)

    def finish(q):
        total = own[q]
        for s in range(1, G):
            u_copy(q, s).wait_recv()
            total = total + urecv[q, s - 1]
        mine = img[q, :, :, pl.ds(pl.multiple_of(a * share, share), share)]
        new = mine.reshape(rows, share).astype(jnp.float32) + total * own_inv
        newv[q] = new.reshape(G, kc, share)
        for cp in new_copies(q):
            cp.start()

    forward_on(0)
    pltpu.make_async_copy(crecv, crecv, crecv_sem).wait()
    columns = colp[a][:1]
    for s in range(1, G):
        columns = columns + crecv[s - 1][:1]
    own_inv = 1.0 / columns
    for q in range(NC):
        process(q)
        if q + 1 < NC:
            forward_on(q + 1)
        if q >= 1:
            finish(q - 1)
    finish(NC - 1)

    pltpu.make_async_copy(
        proj.at[0, pl.ds(0, C - 1)], proj.at[0, pl.ds(0, C - 1)], send_sem
    ).wait()
    for s in range(1, G):
        pltpu.make_async_remote_copy(
            src_ref=colp.at[0], dst_ref=crecv.at[s - 1], send_sem=csend_sem.at[s - 1],
            recv_sem=crecv_sem, device_id=(c, lax.rem(a + s, G)), device_id_type=MESH,
        ).wait_send()
    for q in range(NC):
        for s in range(1, G):
            u_copy(q, s).wait_send()
            pltpu.make_async_copy(
                hop.at[q, pl.ds(0, T)], hop.at[q, pl.ds(0, T)], fwd_sem.at[q, s - 1]
            ).wait()
        for cp in res_copies(q) + new_copies(q):
            cp.wait()


def on_device(C, G, projections, start_image, system, first_tile):
    T = C // G
    KR = projections.shape[3]
    NC = max(1, min(MAX_CHUNKS, KR // 16))
    kc = KR // NC
    rows = G * kc
    slices, npix = start_image.shape
    bins = projections.shape[4]
    share = npix // G
    bf16, f32 = jnp.bfloat16, jnp.float32
    dma = pltpu.SemaphoreType.DMA
    hbm = pl.BlockSpec(memory_space=pl.ANY)
    return pl.pallas_call(
        functools.partial(kernel, C, G, NC),
        out_shape=(
            jax.ShapeDtypeStruct((slices, share), f32),
            jax.ShapeDtypeStruct((T, slices, bins), bf16),
        ),
        in_specs=[pl.BlockSpec(memory_space=pltpu.SMEM), hbm, hbm, hbm],
        out_specs=(hbm, hbm),
        scratch_shapes=[
            pltpu.VMEM((NC, G, kc, npix), bf16),
            pltpu.VMEM(system.shape, bf16),
            pltpu.VMEM((T, npix, bins), bf16),
            pltpu.VMEM((T, NC * rows, bins), f32),
            pltpu.VMEM((T, 8, bins), f32),
            pltpu.VMEM((NC, C, kc, bins), bf16),
            pltpu.VMEM((NC, G - 1, T, kc, bins), bf16),
            pltpu.VMEM((NC, T, G, kc, bins), bf16),
            pltpu.VMEM((NC, G - 1, rows, share), f32),
            pltpu.VMEM((NC, rows, share), f32),
            pltpu.VMEM((NC, G - 1, rows, share), f32),
            pltpu.VMEM((G, 8, share), f32),
            pltpu.VMEM((G - 1, 8, share), f32),
            pltpu.VMEM((NC, G, kc, share), f32),
            dma((NC, G)),
            dma,
            dma,
            dma((NC,)),
            dma((NC, G - 1)),
            dma((NC, G - 1)),
            dma((NC, G - 1)),
            dma((NC, G - 1)),
            dma((G - 1,)),
            dma,
            dma((NC, G)),
            dma((NC, G)),
        ],
        compiler_params=pltpu.CompilerParams(
            collective_id=0, has_side_effects=True, vmem_limit_bytes=48 * 1024 * 1024
        ),
    )(first_tile, projections, start_image, system)


def solution(mesh):
    in_specs = (
        P("cuts", None, "ang", None, None),
        P("cuts", None),
        P("ang", None, None, None, None),
        P("ang", None),
    )
    out_specs = (P("cuts", "ang"), P("ang", "cuts", None))
    return jax.shard_map(
        functools.partial(on_device, mesh.shape["cuts"], mesh.shape["ang"]),
        mesh=mesh, in_specs=in_specs, out_specs=out_specs, check_vma=False,
    )
```

time: 124 us -> 56.8 us (0.46)
  the two profiles are of different devices: /device:TPU:0 before, /device:TPU:10 now
where the time goes in v1:
time: 56.8 us; the launch traced here: 56.6 us
  Pallas kernels  49.6 us (87%)
  local copies, waits for them, and re-layouts  6.3 us (11%)
  between operations  0.65 us (1%)
    pallas_call x1, Pallas kernels, on_device(): pl.pallas_call(functools.partial(kernel, C, G, NC), out_shape=(jax.ShapeD...  49.6 us
    unnamed x10, local copies, waits for them, and re-layouts  6.3 us

profile of v1, /device:TPU:10, one launch (start us, length us, event | category | flops | bytes accessed | tf_op | source)
XLA Modules:
  0.0 56.6 jit_solution(6394409223538057532)
XLA Ops:
  0.6 0.0 copy-start
  0.6 1.6 %copy-done = bf16[4,16,2,64,128]{4,3,2,1,0:T(8,128)(2,1)S(1)} copy-done((bf16[4,16,2,64,128]{4,3,2,1,0:T(8,128)(2,1)S(1)}, bf16[4,16,2,64,128]{4,3,2,1,0:T(8,128)(2,1)}, u32[]{:S(2)}) %copy-start) | copy-done | bytes 2097176
  2.2 0.0 copy-start.1
  2.2 1.2 %copy-done.1 = bf16[1,16,1,128,256]{4,3,2,1,0:T(8,128)(2,1)S(1)} copy-done((bf16[1,16,1,128,256]{4,3,2,1,0:T(8,128)(2,1)S(1)}, bf16[1,16,1,128,256]{4,3,2,1,0:T(8,128)(2,1)}, u32[]{:S(2)}) %copy-start.1) | copy-done | bytes 1048600
  3.4 0.0 copy-start.2
  3.5 1.0 %copy-done.2 = bf16[256,1024]{1,0:T(8,128)(2,1)S(1)} copy-done((bf16[256,1024]{1,0:T(8,128)(2,1)S(1)}, bf16[256,1024]{1,0:T(8,128)(2,1)}, u32[]{:S(2)}) %copy-start.2) | copy-done | bytes 524312
  4.5 0.0 copy-start.3
  4.5 0.7 %copy-done.3 = s32[4,16]{1,0:T(4,128)S(1)} copy-done((s32[4,16]{1,0:T(4,128)S(1)}, s32[4,16]{1,0:T(4,128)}, u32[]{:S(2)}) %copy-start.3) | copy-done | bytes 280
  5.2 49.6 %shard_map.59 = (f32[256,512]{1,0:T(8,128)S(1)}, bf16[8,256,256]{2,1,0:T(8,128)(2,1)S(1)}) custom-call(s32[4,16]{1,0:T(4,128)S(1)} %copy-done.3, bf16[1,16,1,128,256]{4,3,2,1,0:T(8,128)(2,1)S(1)} %copy-done.1, bf16[256,1024]{1,0:T(8,128)(2,1)S(1)} %copy-done.2, bf16[4,16,2,64,128]{4,3,2,1,0:T(8,128)(2,1)S(1)} %copy-done), custom_call_target="tpu_custom_call" | custom-call | tf_op jit(solution)/shard_map/pallas_call | solution.py:239
  54.8 0.8 %copy.8 = f32[256,512]{1,0:T(8,128)} copy(f32[256,512]{1,0:T(8,128)S(1)} %get-tuple-element.4) | data formatting | bytes 1048576
  55.6 1.0 %copy.9 = bf16[8,256,256]{2,1,0:T(8,128)(2,1)} copy(bf16[8,256,256]{2,1,0:T(8,128)(2,1)S(1)} %get-tuple-element.5) | data formatting | bytes 2097152
Async XLA Ops:
  0.6 1.6 %copy-start = (bf16[4,16,2,64,128]{4,3,2,1,0:T(8,128)(2,1)S(1)}, bf16[4,16,2,64,128]{4,3,2,1,0:T(8,128)(2,1)}, u32[]{:S(2)}) copy-start(bf16[4,16,2,64,128]{4,3,2,1,0:T(8,128)(2,1)} %system.1) | copy-start | bytes 6291460
  2.2 1.2 %copy-start.1 = (bf16[1,16,1,128,256]{4,3,2,1,0:T(8,128)(2,1)S(1)}, bf16[1,16,1,128,256]{4,3,2,1,0:T(8,128)(2,1)}, u32[]{:S(2)}) copy-start(bf16[1,16,1,128,256]{4,3,2,1,0:T(8,128)(2,1)} %proj.1) | copy-start | bytes 3145732
  3.4 1.0 %copy-start.2 = (bf16[256,1024]{1,0:T(8,128)(2,1)S(1)}, bf16[256,1024]{1,0:T(8,128)(2,1)}, u32[]{:S(2)}) copy-start(bf16[256,1024]{1,0:T(8,128)(2,1)} %image.1) | copy-start | bytes 1572868
  4.5 0.7 %copy-start.3 = (s32[4,16]{1,0:T(4,128)S(1)}, s32[4,16]{1,0:T(4,128)}, u32[]{:S(2)}) copy-start(s32[4,16]{1,0:T(4,128)} %first.1) | copy-start | bytes 772

commit v2 on v1

--- a/solution.py
+++ b/solution.py
@@ -13,9 +13,9 @@
 
 
 def kernel(
-    C, G, NC, first, proj, image, system, new_out, res_out,
-    img, sysv, A, F, inv, hop, arr, R, U, own, urecv, colp, crecv, newv,
-    img_sem, sys_sem, send_sem, hop_sem, fwd_sem, arr_sem,
+    C, G, NC, first_in, proj, image, system, new_out, res_out,
+    first, img, sysv, A, F, inv, arr, R, U, own, urecv, colp, crecv, newv,
+    first_sem, img_sem, sys_sem, send_sem, arr_sem,
     usend_sem, urecv_sem, csend_sem, crecv_sem, res_sem, new_sem,
 ):
     c = lax.axis_index("cuts")
@@ -31,14 +31,30 @@
     half = bins // PW
     ntiles = bins // W
 
+    tgt = c // T
+    slot = a * T + lax.rem(c, T)
+
     barrier = pltpu.get_barrier_semaphore()
-    for s in range(1, C):
-        pl.semaphore_signal(barrier, inc=1, device_id=(lax.rem(c + s, C), a), device_id_type=MESH)
+    for i in range(T):
+        source = a * T + lax.rem(c + i, T)
+        for s in range(1 if i == 0 else 0, G):
+            pl.semaphore_signal(
+                barrier, inc=1, device_id=(source, lax.rem(a + s, G)), device_id_type=MESH
+            )
+
+    @pl.when(tgt != a)
+    def _():
+        pl.semaphore_signal(
+            barrier, inc=1, device_id=(a * T + lax.rem(c, T), a), device_id_type=MESH
+        )
+
     for s in range(1, G):
         pl.semaphore_signal(barrier, inc=1, device_id=(c, lax.rem(a + s, G)), device_id_type=MESH)
 
     sys_copy = pltpu.make_async_copy(system, sysv, sys_sem)
     sys_copy.start()
+    first_copy = pltpu.make_async_copy(first_in, first, first_sem)
+    first_copy.start()
     img_copies = []
     for q in range(NC):
         for b in range(G):
@@ -47,26 +63,34 @@
             )
             cp.start()
             img_copies.append(cp)
-    for q in range(NC):
-        pltpu.make_async_copy(
-            proj.at[0, c, 0, pl.ds(q * kc, kc)], hop.at[q, c], hop_sem.at[q]
-        ).start()
-
-    pl.semaphore_wait(barrier, C - 1 + G - 1)
+    pl.semaphore_wait(barrier, C + G - 1 - jnp.where(tgt == a, 1, 0))
+
+    def piece(q, o):
+        return pltpu.make_async_remote_copy(
+            src_ref=proj.at[0, o, 0, pl.ds(q * kc, kc)],
+            dst_ref=arr.at[q, slot],
+            send_sem=send_sem,
+            recv_sem=arr_sem.at[q],
+            device_id=(o, tgt),
+            device_id_type=MESH,
+        )
 
     for q in range(NC):
         for s in range(1, C):
-            o = lax.rem(c + s, C)
-            pltpu.make_async_remote_copy(
-                src_ref=proj.at[0, o, 0, pl.ds(q * kc, kc)],
-                dst_ref=hop.at[q, c],
-                send_sem=send_sem,
-                recv_sem=hop_sem.at[q],
-                device_id=(o, a),
-                device_id_type=MESH,
+            piece(q, lax.rem(c + s, C)).start()
+
+        @pl.when(tgt != a)
+        def _(q=q):
+            piece(q, c).start()
+
+        @pl.when(tgt == a)
+        def _(q=q):
+            pltpu.make_async_copy(
+                proj.at[0, c, 0, pl.ds(q * kc, kc)], arr.at[q, slot], arr_sem.at[q]
             ).start()
 
     sys_copy.wait()
+    first_copy.wait()
 
 
     def build(p, carry):
@@ -114,19 +138,6 @@
             recv_sem=crecv_sem, device_id=(c, g), device_id_type=MESH,
         ).start()
 
-    def forward_on(q):
-        pltpu.make_async_copy(hop.at[q], hop.at[q], hop_sem.at[q]).wait()
-        for s in range(1, G):
-            g = lax.rem(a + s, G)
-            pltpu.make_async_remote_copy(
-                src_ref=hop.at[q, pl.ds(g * T, T)],
-                dst_ref=arr.at[q, s - 1],
-                send_sem=fwd_sem.at[q, s - 1],
-                recv_sem=arr_sem.at[q, s - 1],
-                device_id=(c, g),
-                device_id_type=MESH,
-            ).start()
-
     def res_copies(q):
         out = []
         for b in range(G):
@@ -143,11 +154,13 @@
             for b in range(G)
         ]
 
-    def residual_part(q, b, source):
+    def residual_part(q):
         def body(t, carry):
-            value = source(t).astype(jnp.float32)
-            f = F[t, pl.ds(pl.multiple_of(q * rows + b * kc, kc), kc)]
-            R[q, t, b] = ((value - f) * inv[t][:1]).astype(jnp.bfloat16)
+            scale = inv[t][:1]
+            for b in range(G):
+                value = arr[q, b * T + t].astype(jnp.float32)
+                f = F[t, pl.ds(q * rows + b * kc, kc)]
+                R[q, t, b] = ((value - f) * scale).astype(jnp.bfloat16)
             return carry
 
         lax.fori_loop(0, T, body, 0)
@@ -170,10 +183,8 @@
         )
 
     def process(q):
-        residual_part(q, a, lambda t: hop[q, a * T + t])
-        for s in range(1, G):
-            pltpu.make_async_copy(arr.at[q, s - 1], arr.at[q, s - 1], arr_sem.at[q, s - 1]).wait()
-            residual_part(q, lax.rem(a + G - s, G), lambda t, s=s: arr[q, s - 1, t])
+        pltpu.make_async_copy(arr.at[q], arr.at[q], arr_sem.at[q]).wait()
+        residual_part(q)
         for cp in res_copies(q):
             cp.start()
         for s in range(1, G):
@@ -192,7 +203,6 @@
         for cp in new_copies(q):
             cp.start()
 
-    forward_on(0)
     pltpu.make_async_copy(crecv, crecv, crecv_sem).wait()
     columns = colp[a][:1]
     for s in range(1, G):
@@ -200,15 +210,19 @@
     own_inv = 1.0 / columns
     for q in range(NC):
         process(q)
-        if q + 1 < NC:
-            forward_on(q + 1)
         if q >= 1:
             finish(q - 1)
     finish(NC - 1)
 
-    pltpu.make_async_copy(
-        proj.at[0, pl.ds(0, C - 1)], proj.at[0, pl.ds(0, C - 1)], send_sem
-    ).wait()
+    @pl.when(tgt == a)
+    def _():
+        sent = proj.at[0, pl.ds(0, C - 1)]
+        pltpu.make_async_copy(sent, sent, send_sem).wait()
+
+    @pl.when(tgt != a)
+    def _():
+        pltpu.make_async_copy(proj.at[0], proj.at[0], send_sem).wait()
+
     for s in range(1, G):
         pltpu.make_async_remote_copy(
             src_ref=colp.at[0], dst_ref=crecv.at[s - 1], send_sem=csend_sem.at[s - 1],
@@ -217,9 +231,6 @@
     for q in range(NC):
         for s in range(1, G):
             u_copy(q, s).wait_send()
-            pltpu.make_async_copy(
-                hop.at[q, pl.ds(0, T)], hop.at[q, pl.ds(0, T)], fwd_sem.at[q, s - 1]
-            ).wait()
         for cp in res_copies(q) + new_copies(q):
             cp.wait()
 
@@ -242,16 +253,16 @@
             jax.ShapeDtypeStruct((slices, share), f32),
             jax.ShapeDtypeStruct((T, slices, bins), bf16),
         ),
-        in_specs=[pl.BlockSpec(memory_space=pltpu.SMEM), hbm, hbm, hbm],
+        in_specs=[pl.BlockSpec(memory_space=pltpu.HBM)] * 4,
         out_specs=(hbm, hbm),
         scratch_shapes=[
+            pltpu.SMEM(first_tile.shape, jnp.int32),
             pltpu.VMEM((NC, G, kc, npix), bf16),
             pltpu.VMEM(system.shape, bf16),
             pltpu.VMEM((T, npix, bins), bf16),
             pltpu.VMEM((T, NC * rows, bins), f32),
             pltpu.VMEM((T, 8, bins), f32),
             pltpu.VMEM((NC, C, kc, bins), bf16),
-            pltpu.VMEM((NC, G - 1, T, kc, bins), bf16),
             pltpu.VMEM((NC, T, G, kc, bins), bf16),
             pltpu.VMEM((NC, G - 1, rows, share), f32),
             pltpu.VMEM((NC, rows, share), f32),
@@ -259,12 +270,11 @@
             pltpu.VMEM((G, 8, share), f32),
             pltpu.VMEM((G - 1, 8, share), f32),
             pltpu.VMEM((NC, G, kc, share), f32),
+            dma,
             dma((NC, G)),
             dma,
             dma,
             dma((NC,)),
-            dma((NC, G - 1)),
-            dma((NC, G - 1)),
             dma((NC, G - 1)),
             dma((NC, G - 1)),
             dma((G - 1,)),
@@ -273,7 +283,7 @@
             dma((NC, G)),
         ],
         compiler_params=pltpu.CompilerParams(
-            collective_id=0, has_side_effects=True, vmem_limit_bytes=48 * 1024 * 1024
+            collective_id=0, has_side_effects=True, vmem_limit_bytes=63 * 1024 * 1024
         ),
     )(first_tile, projections, start_image, system)
 

time: 56.8 us -> 43.3 us (0.76)
  the two profiles are of different devices: /device:TPU:10 before, /device:TPU:0 now
where the time goes in v2:
time: 43.3 us; the launch traced here: 43.1 us
  Pallas kernels  38.3 us (88%)
  local copies, waits for them, and re-layouts  4.13 us (10%)
  between operations  0.64 us (1%)
    pallas_call x1, Pallas kernels, on_device(): pl.pallas_call(functools.partial(kernel, C, G, NC), out_shape=(jax.ShapeD...  38.3 us
    unnamed x2, local copies, waits for them, and re-layouts  4.13 us

profile of v2, /device:TPU:0, one launch (start us, length us, event | category | flops | bytes accessed | tf_op | source)
XLA Modules:
  0.0 43.1 jit_solution(5167877139833962014)
XLA Ops:
  0.6 38.3 %shard_map.59 = (f32[256,512]{1,0:T(8,128)}, bf16[8,256,256]{2,1,0:T(8,128)(2,1)}) custom-call(s32[4,16]{1,0:T(4,128)} %first_in.1, bf16[1,16,1,128,256]{4,3,2,1,0:T(8,128)(2,1)} %proj.1, bf16[256,1024]{1,0:T(8,128)(2,1)} %image.1, bf16[4,16,2,64,128]{4,3,2,1,0:T(8,128)(2,1)} %system.1), custom_call_target="tpu_custom_call" | custom-call | tf_op jit(solution)/shard_map/pallas_call | solution.py:250
  39.0 1.9 %copy.8 = f32[256,512]{1,0:T(8,128)} copy(f32[256,512]{1,0:T(8,128)} %get-tuple-element.4) | data formatting | bytes 1048576
  40.8 2.3 %copy.9 = bf16[8,256,256]{2,1,0:T(8,128)(2,1)} copy(bf16[8,256,256]{2,1,0:T(8,128)(2,1)} %get-tuple-element.5) | data formatting | bytes 2097152

commit v3 on v2

--- a/solution.py
+++ b/solution.py
@@ -9,22 +9,23 @@
 
 MESH = pl.DeviceIdType.MESH
 NT = (((1,), (1,)), ((), ()))
-MAX_CHUNKS = 4
+SPLIT = (3, 3, 2)
+VMEM_BYTES = 67043328 - 0
 
 
 def kernel(
-    C, G, NC, first_in, proj, image, system, new_out, res_out,
-    first, img, sysv, A, F, inv, arr, R, U, own, urecv, colp, crecv, newv,
+    C, G, sizes, first_in, proj, image, system, new_out, res_out,
+    first, img, sysv, A, F, inv, arr, R, U, own, urecv, colp, crecv,
     first_sem, img_sem, sys_sem, send_sem, arr_sem,
-    usend_sem, urecv_sem, csend_sem, crecv_sem, res_sem, new_sem,
+    usend_sem, urecv_sem, csend_sem, crecv_sem,
 ):
     c = lax.axis_index("cuts")
     a = lax.axis_index("ang")
     T = C // G
     blocks, ptiles, _, W, PW = system.shape
     KR = proj.shape[3]
-    kc = KR // NC
-    rows = G * kc
+    NC = len(sizes)
+    starts = [sum(sizes[:q]) for q in range(NC)]
     npix = image.shape[1]
     share = npix // G
     bins = proj.shape[4]
@@ -59,7 +60,9 @@
     for q in range(NC):
         for b in range(G):
             cp = pltpu.make_async_copy(
-                image.at[pl.ds(b * KR + q * kc, kc)], img.at[q, b], img_sem.at[q, b]
+                image.at[pl.ds(b * KR + starts[q], sizes[q])],
+                img.at[pl.ds(G * starts[q] + b * sizes[q], sizes[q])],
+                img_sem.at[q, b],
             )
             cp.start()
             img_copies.append(cp)
@@ -67,8 +70,8 @@
 
     def piece(q, o):
         return pltpu.make_async_remote_copy(
-            src_ref=proj.at[0, o, 0, pl.ds(q * kc, kc)],
-            dst_ref=arr.at[q, slot],
+            src_ref=proj.at[0, o, 0, pl.ds(starts[q], sizes[q])],
+            dst_ref=arr[q].at[slot],
             send_sem=send_sem,
             recv_sem=arr_sem.at[q],
             device_id=(o, tgt),
@@ -86,7 +89,7 @@
         @pl.when(tgt == a)
         def _(q=q):
             pltpu.make_async_copy(
-                proj.at[0, c, 0, pl.ds(q * kc, kc)], arr.at[q, slot], arr_sem.at[q]
+                proj.at[0, c, 0, pl.ds(starts[q], sizes[q])], arr[q].at[slot], arr_sem.at[q]
             ).start()
 
     sys_copy.wait()
@@ -118,7 +121,7 @@
     def project(t, carry):
         m = A[t]
         F[t] = jnp.dot(
-            img[...].reshape(NC * rows, npix), m, preferred_element_type=jnp.float32
+            img[...], m, preferred_element_type=jnp.float32
         )
         ones_r = jnp.ones((16, npix), jnp.bfloat16)
         ones_b = jnp.ones((16, bins), jnp.bfloat16)
@@ -138,70 +141,55 @@
             recv_sem=crecv_sem, device_id=(c, g), device_id_type=MESH,
         ).start()
 
-    def res_copies(q):
-        out = []
-        for b in range(G):
-            out.append(pltpu.make_async_copy(
-                R.at[q, :, b], res_out.at[:, pl.ds(b * KR + q * kc, kc)], res_sem.at[q, b]
-            ))
-        return out
-
-    def new_copies(q):
-        return [
-            pltpu.make_async_copy(
-                newv.at[q, b], new_out.at[pl.ds(b * KR + q * kc, kc)], new_sem.at[q, b]
-            )
-            for b in range(G)
-        ]
-
     def residual_part(q):
         def body(t, carry):
             scale = inv[t][:1]
             for b in range(G):
-                value = arr[q, b * T + t].astype(jnp.float32)
-                f = F[t, pl.ds(q * rows + b * kc, kc)]
-                R[q, t, b] = ((value - f) * scale).astype(jnp.bfloat16)
+                value = arr[q][b * T + t].astype(jnp.float32)
+                f = F[t, pl.ds(G * starts[q] + b * sizes[q], sizes[q])]
+                res = ((value - f) * scale).astype(jnp.bfloat16)
+                R[q][t, pl.ds(b * sizes[q], sizes[q])] = res
+                res_out[t, pl.ds(b * KR + starts[q], sizes[q])] = res
             return carry
 
         lax.fori_loop(0, T, body, 0)
 
     def back(q, g):
-        total = jnp.zeros((rows, share), jnp.float32)
+        total = jnp.zeros((G * sizes[q], share), jnp.float32)
         pix = pl.ds(pl.multiple_of(g * share, share), share)
         for t in range(T):
             total = total + lax.dot_general(
-                R[q, t].reshape(rows, bins), A[t, pix], NT, preferred_element_type=jnp.float32
+                R[q][t], A[t, pix], NT, preferred_element_type=jnp.float32
             )
         return total
 
     def u_copy(q, s):
         g = lax.rem(a + s, G)
         return pltpu.make_async_remote_copy(
-            src_ref=U.at[q, s - 1], dst_ref=urecv.at[q, s - 1],
+            src_ref=U[q].at[s - 1], dst_ref=urecv[q].at[s - 1],
             send_sem=usend_sem.at[q, s - 1], recv_sem=urecv_sem.at[q, s - 1],
             device_id=(c, g), device_id_type=MESH,
         )
 
     def process(q):
-        pltpu.make_async_copy(arr.at[q], arr.at[q], arr_sem.at[q]).wait()
+        pltpu.make_async_copy(arr[q], arr[q], arr_sem.at[q]).wait()
         residual_part(q)
-        for cp in res_copies(q):
-            cp.start()
         for s in range(1, G):
-            U[q, s - 1] = back(q, lax.rem(a + s, G))
+            U[q][s - 1] = back(q, lax.rem(a + s, G))
             u_copy(q, s).start()
-        own[q] = back(q, a)
+        own[q][...] = back(q, a)
 
     def finish(q):
-        total = own[q]
+        total = own[q][...]
         for s in range(1, G):
             u_copy(q, s).wait_recv()
-            total = total + urecv[q, s - 1]
-        mine = img[q, :, :, pl.ds(pl.multiple_of(a * share, share), share)]
-        new = mine.reshape(rows, share).astype(jnp.float32) + total * own_inv
-        newv[q] = new.reshape(G, kc, share)
-        for cp in new_copies(q):
-            cp.start()
+            total = total + urecv[q][s - 1]
+        mine = img[
+            pl.ds(G * starts[q], G * sizes[q]), pl.ds(pl.multiple_of(a * share, share), share)
+        ]
+        new = mine.astype(jnp.float32) + total * own_inv
+        for b in range(G):
+            new_out[pl.ds(b * KR + starts[q], sizes[q])] = new[b * sizes[q] : (b + 1) * sizes[q]]
 
     pltpu.make_async_copy(crecv, crecv, crecv_sem).wait()
     columns = colp[a][:1]
@@ -231,45 +219,49 @@
     for q in range(NC):
         for s in range(1, G):
             u_copy(q, s).wait_send()
-        for cp in res_copies(q) + new_copies(q):
-            cp.wait()
+
+
+def chunk_sizes(rows):
+    unit = max(16, rows // sum(SPLIT))
+    sizes = [n * unit for n in SPLIT]
+    if sum(sizes) == rows:
+        return sizes
+    return [16] * (rows // 16) if rows % 16 == 0 else [rows]
 
 
 def on_device(C, G, projections, start_image, system, first_tile):
     T = C // G
     KR = projections.shape[3]
-    NC = max(1, min(MAX_CHUNKS, KR // 16))
-    kc = KR // NC
-    rows = G * kc
+    sizes = chunk_sizes(KR)
+    NC = len(sizes)
     slices, npix = start_image.shape
     bins = projections.shape[4]
     share = npix // G
     bf16, f32 = jnp.bfloat16, jnp.float32
     dma = pltpu.SemaphoreType.DMA
-    hbm = pl.BlockSpec(memory_space=pl.ANY)
+    out_bytes = slices * share * 4 + T * slices * bins * 2
     return pl.pallas_call(
-        functools.partial(kernel, C, G, NC),
+        functools.partial(kernel, C, G, sizes),
         out_shape=(
-            jax.ShapeDtypeStruct((slices, share), f32),
-            jax.ShapeDtypeStruct((T, slices, bins), bf16),
+            pltpu.VMEM((slices, share), f32),
+            pltpu.VMEM((T, slices, bins), bf16),
         ),
         in_specs=[pl.BlockSpec(memory_space=pltpu.HBM)] * 4,
-        out_specs=(hbm, hbm),
+        out_specs=(pl.BlockSpec(memory_space=pltpu.VMEM),) * 2,
         scratch_shapes=[
             pltpu.SMEM(first_tile.shape, jnp.int32),
-            pltpu.VMEM((NC, G, kc, npix), bf16),
+            pltpu.VMEM((slices, npix), bf16),
             pltpu.VMEM(system.shape, bf16),
             pltpu.VMEM((T, npix, bins), bf16),
-            pltpu.VMEM((T, NC * rows, bins), f32),
+            pltpu.VMEM((T, slices, bins), f32),
             pltpu.VMEM((T, 8, bins), f32),
-            pltpu.VMEM((NC, C, kc, bins), bf16),
-            pltpu.VMEM((NC, T, G, kc, bins), bf16),
-            pltpu.VMEM((NC, G - 1, rows, share), f32),
-            pltpu.VMEM((NC, rows, share), f32),
-            pltpu.VMEM((NC, G - 1, rows, share), f32),
+            [pltpu.VMEM((C, n, bins), bf16) for n in sizes],
+            [pltpu.VMEM((T, G * n, bins), bf16) for n in sizes],
+            [pltpu.VMEM((G - 1, G * n, share), f32) for n in sizes],
+            [pltpu.VMEM((G * n, share), f32) for n in sizes],
+            [pltpu.VMEM((G - 1, G * n, share), f32) for n in sizes],
             pltpu.VMEM((G, 8, share), f32),
             pltpu.VMEM((G - 1, 8, share), f32),
-            pltpu.VMEM((NC, G, kc, share), f32),
             dma,
             dma((NC, G)),
             dma,
@@ -279,11 +271,9 @@
             dma((NC, G - 1)),
             dma((G - 1,)),
             dma,
-            dma((NC, G)),
-            dma((NC, G)),
         ],
         compiler_params=pltpu.CompilerParams(
-            collective_id=0, has_side_effects=True, vmem_limit_bytes=63 * 1024 * 1024
+            collective_id=0, has_side_effects=True, vmem_limit_bytes=VMEM_BYTES - out_bytes
         ),
     )(first_tile, projections, start_image, system)
 

time: 43.3 us -> 39.1 us (0.903)
  local copies, waits for them, and re-layouts: 4.13 us -> 1.77 us
  Pallas kernels: 38.3 us -> 36.1 us
    unnamed x2, local copies, waits for them, and re-layouts: 4.13 us -> 1.77 us
    pallas_call x1, Pallas kernels: 38.3 us -> 36.1 us  [on_device(): pl.pallas_call(functools.partial(kernel, C, G, sizes), out_shape=(pltpu.V...]
where the time goes in v3:
time: 39.1 us; the launch traced here: 38.5 us
  Pallas kernels  36.1 us (92%)
  local copies, waits for them, and re-layouts  1.77 us (5%)
  between operations  0.64 us (2%)
    pallas_call x1, Pallas kernels, on_device(): pl.pallas_call(functools.partial(kernel, C, G, sizes), out_shape=(pltpu.V...  36.1 us
    unnamed x2, local copies, waits for them, and re-layouts  1.77 us

profile of v3, /device:TPU:0, one launch (start us, length us, event | category | flops | bytes accessed | tf_op | source)
XLA Modules:
  0.0 38.5 jit_solution(3467817282757288887)
XLA Ops:
  0.6 36.1 %shard_map.59 = (f32[256,512]{1,0:T(8,128)S(1)}, bf16[8,256,256]{2,1,0:T(8,128)(2,1)S(1)}) custom-call(s32[4,16]{1,0:T(4,128)} %first_in.1, bf16[1,16,1,128,256]{4,3,2,1,0:T(8,128)(2,1)} %proj.1, bf16[256,1024]{1,0:T(8,128)(2,1)} %image.1, bf16[4,16,2,64,128]{4,3,2,1,0:T(8,128)(2,1)} %system.1), custom_call_target="tpu_custom_call" | custom-call | tf_op jit(solution)/shard_map/pallas_call | solution.py:243
  36.7 0.8 %copy.8 = f32[256,512]{1,0:T(8,128)} copy(f32[256,512]{1,0:T(8,128)S(1)} %get-tuple-element.2) | data formatting | bytes 1048576
  37.5 1.0 %copy.9 = bf16[8,256,256]{2,1,0:T(8,128)(2,1)} copy(bf16[8,256,256]{2,1,0:T(8,128)(2,1)S(1)} %get-tuple-element.3) | data formatting | bytes 2097152

commit v4 on v3

--- a/solution.py
+++ b/solution.py
@@ -10,6 +10,7 @@
 MESH = pl.DeviceIdType.MESH
 NT = (((1,), (1,)), ((), ()))
 SPLIT = (3, 3, 2)
+PUTS = 4
 VMEM_BYTES = 67043328 - 0
 
 
@@ -221,6 +222,19 @@
             u_copy(q, s).wait_send()
 
 
+def put_out(new_in, res_in, new_out, res_out, sem):
+    copies = []
+    for i, (src, dst) in enumerate(((new_in, new_out), (res_in, res_out))):
+        n = src.shape[0] // PUTS
+        for k in range(PUTS):
+            part = pl.ds(k * n, n)
+            copies.append(pltpu.make_async_copy(src.at[part], dst.at[part], sem.at[i * PUTS + k]))
+    for cp in copies:
+        cp.start()
+    for cp in copies:
+        cp.wait()
+
+
 def chunk_sizes(rows):
     unit = max(16, rows // sum(SPLIT))
     sizes = [n * unit for n in SPLIT]
@@ -240,7 +254,7 @@
     bf16, f32 = jnp.bfloat16, jnp.float32
     dma = pltpu.SemaphoreType.DMA
     out_bytes = slices * share * 4 + T * slices * bins * 2
-    return pl.pallas_call(
+    new_image, residual = pl.pallas_call(
         functools.partial(kernel, C, G, sizes),
         out_shape=(
             pltpu.VMEM((slices, share), f32),
@@ -276,6 +290,17 @@
             collective_id=0, has_side_effects=True, vmem_limit_bytes=VMEM_BYTES - out_bytes
         ),
     )(first_tile, projections, start_image, system)
+    return pl.pallas_call(
+        put_out,
+        out_shape=(
+            jax.ShapeDtypeStruct(new_image.shape, f32),
+            jax.ShapeDtypeStruct(residual.shape, bf16),
+        ),
+        in_specs=[pl.BlockSpec(memory_space=pl.ANY)] * 2,
+        out_specs=(pl.BlockSpec(memory_space=pl.ANY),) * 2,
+        scratch_shapes=[dma((2 * PUTS,))],
+        compiler_params=pltpu.CompilerParams(vmem_limit_bytes=1 << 20),
+    )(new_image, residual)
 
 
 def solution(mesh):

time: 39.1 us -> 38.5 us (0.985)
  local copies, waits for them, and re-layouts: 1.77 us -> 0 us
  Pallas kernels: 36.1 us -> 37.3 us
    unnamed x2 -> x0, local copies, waits for them, and re-layouts: 1.77 us -> none
    pallas_call x0 -> x1, Pallas kernels: none -> 1.21 us  [on_device(): pl.pallas_call(put_out, out_shape=(jax.ShapeDtypeStruct(new_image.shape,...]
where the time goes in v4:
time: 38.5 us; the launch traced here: 37.9 us
  Pallas kernels  37.3 us (97%)
  between operations  0.64 us (2%)
    pallas_call x1, Pallas kernels, on_device(): pl.pallas_call(functools.partial(kernel, C, G, sizes), out_shape=(pltpu.V...  36.1 us
    pallas_call x1, Pallas kernels, on_device(): pl.pallas_call(put_out, out_shape=(jax.ShapeDtypeStruct(new_image.shape,...  1.21 us

profile of v4, /device:TPU:0, one launch (start us, length us, event | category | flops | bytes accessed | tf_op | source)
XLA Modules:
  0.0 37.9 jit_solution(6036984188709287909)
XLA Ops:
  0.6 36.1 %shard_map.59 = (f32[256,512]{1,0:T(8,128)S(1)}, bf16[8,256,256]{2,1,0:T(8,128)(2,1)S(1)}) custom-call(s32[4,16]{1,0:T(4,128)} %first_in.1, bf16[1,16,1,128,256]{4,3,2,1,0:T(8,128)(2,1)} %proj.1, bf16[256,1024]{1,0:T(8,128)(2,1)} %image.1, bf16[4,16,2,64,128]{4,3,2,1,0:T(8,128)(2,1)} %system.1), custom_call_target="tpu_custom_call" | custom-call | tf_op jit(solution)/shard_map/pallas_call | solution.py:257
  36.7 1.2 %shard_map.60 = (f32[256,512]{1,0:T(8,128)}, bf16[8,256,256]{2,1,0:T(8,128)(2,1)}) custom-call(f32[256,512]{1,0:T(8,128)S(1)} %get-tuple-element.4.new_in, bf16[8,256,256]{2,1,0:T(8,128)(2,1)S(1)} %get-tuple-element.5.res_in), custom_call_target="tpu_custom_call" | custom-call | tf_op jit(solution)/shard_map/pallas_call | solution.py:293
